TPU v7x, 32 devices: a whole 2x2x4 slice. The times are simulated.
32 devices in a mesh: narrow: 2 (over y), wide: 4 (over z), nys: 4 (over x, core).
Axes of the slice: x: 2, y: 2, z: 4, core: 2. Of those that a mesh axis runs over, the one named last changes fastest.
Arguments:
- centers: bfloat16 [32768, 1024], P(('narrow', 'wide', 'nys')), may hold values from -6 to 6
- weights: float32 [32768, 1000], P(('narrow', 'wide', 'nys')), may hold values from -6 to 6
- batch_points: bfloat16 [512, 1024], P(('narrow', 'wide', 'nys')), may hold values from -6 to 6
- labels: float32 [512, 1000], P(('narrow', 'wide', 'nys')), may hold values from -6 to 6
- nystrom_points: bfloat16 [2048, 1024], P(('narrow', 'nys')), may hold values from -6 to 6
- eigvecs: float32 [2048, 160], P(('narrow', 'nys')), may hold values from -0.125 to 0.125
- corrections: float32 [160], replicated, may hold values from 0.05 to 0.5
Outputs:
- new_weights: float32 [32768, 1000], P(('narrow', 'wide', 'nys'))
All inputs are finite; a program needn't handle non-finite values.
Results may differ from a plain program's by a relative error of at most 0.0003.
The roundings to bfloat16 on the way count: a program that leaves them out, or rounds other values in their place, can miss the bound.
Values may be sent and summed in bfloat16 or wider, within the bound.
No kernel may reach another device: no remote copies, remote signals or barrier semaphores. Data moves between devices by JAX's collectives and lax.ppermute only.
A program may use at most 64 MiB of HBM per device.

v0:
```python
import math
import jax
import jax.numpy as jnp
from jax import lax
from jax.sharding import PartitionSpec as P

BATCH = 512
RATE = 16.0
SPREAD = 4.0


def kernel_with(left, left_sq, right):
    cross = lax.dot_general(
        left, right, (((1,), (1,)), ((), ())), preferred_element_type=jnp.float32
    )
    right_sq = jnp.sum(jnp.square(right.astype(jnp.float32)), axis=1)
    dist = jnp.sqrt(jnp.maximum(left_sq[:, None] + right_sq[None, :] - 2.0 * cross, 0.0))
    radius = math.sqrt(2.0 * left.shape[1])
    return jnp.exp((radius - dist) / SPREAD).astype(jnp.bfloat16)


def squares(points):
    return jnp.sum(jnp.square(points.astype(jnp.float32)), axis=1)


def per_device(centers, weights, batch_points, labels, nystrom_points, eigvecs, corrections):
    batch_all = lax.all_gather(batch_points, ("narrow", "wide", "nys"), axis=0, tiled=True)
    points_all = lax.all_gather(nystrom_points, ("narrow", "nys"), axis=0, tiled=True)
    vectors_full = lax.all_gather(eigvecs, ("narrow", "nys"), axis=0, tiled=True)
    count = lax.axis_size(("narrow", "wide", "nys"))
    scale = (centers.shape[0] * count) ** (-0.5)
    center_sq = squares(centers)
    k_batch = kernel_with(centers, center_sq, batch_all)
    partial_value = (
        lax.dot_general(
            k_batch,
            weights.astype(jnp.bfloat16),
            (((0,), (0,)), ((), ())),
            preferred_element_type=jnp.float32,
        )
        * scale
    )
    rows = labels.shape[0]
    offset = lax.axis_index(("narrow", "wide", "nys")) * rows
    placed = lax.dynamic_update_slice(jnp.zeros_like(partial_value), labels, (offset, jnp.int32(0)))
    residual = lax.psum(partial_value - placed, ("narrow", "wide", "nys")).astype(jnp.bfloat16)
    k_nystrom = kernel_with(nystrom_points, squares(nystrom_points), batch_all)
    pulled = jnp.dot(k_nystrom, residual, preferred_element_type=jnp.float32)
    local_proj = lax.dot_general(
        eigvecs, pulled, (((0,), (0,)), ((), ())), precision=lax.Precision.HIGHEST
    )
    projected = lax.psum(local_proj, ("narrow", "nys"))
    scaled_proj = corrections[:, None] * projected
    gradient = jnp.dot(k_batch, residual, preferred_element_type=jnp.float32)
    corrected_all = jnp.dot(vectors_full, scaled_proj, precision=lax.Precision.HIGHEST).astype(
        jnp.bfloat16
    )
    tile_all = kernel_with(centers, center_sq, points_all)
    nystrom_term = jnp.dot(tile_all, corrected_all, preferred_element_type=jnp.float32)
    return weights - RATE / BATCH * (gradient - nystrom_term)


def solution(mesh):
    placed = (
        P(("narrow", "wide", "nys"), None),
        P(("narrow", "wide", "nys"), None),
        P(("narrow", "wide", "nys"), None),
        P(("narrow", "wide", "nys"), None),
        P(("narrow", "nys"), None),
        P(("narrow", "nys"), None),
        P(),
    )
    return jax.shard_map(
        per_device,
        mesh=mesh,
        in_specs=placed,
        out_specs=P(("narrow", "wide", "nys"), None),
        check_vma=False,
    )
```

profile of v0, /device:TPU:0, one launch (start us, length us, event | category | flops | bytes accessed | tf_op | source)
XLA Modules:
  0.0 260.3 jit_solution(16899667897856393778)
XLA Ops:
  6.5 0.0 all-gather.4.cloned.1.call-start
  6.5 0.7 all-gather.4.cloned.1.call-update
  7.3 0.0 all-gather.8.cloned.1.call-start
  7.3 0.7 all-gather.8.cloned.1.call-update
  8.0 0.0 all-reduce.3.cloned.1.call-start
  8.1 1.2 multiply_reduce_fusion.3
  9.3 2.1 multiply_reduce_fusion.1
  11.4 1.0 copy.8
  12.4 0.2 broadcast_in_dim.2
  12.7 5.5 %dynamic_update_slice.3 = f32[512,1000]{0,1:T(8,128)S(1)} dynamic-update-slice(f32[512,1000]{0,1:T(8,128)S(1)} %broadcast_in_dim.2, f32[16,1000]{0,1:T(8,128)S(1)} %copy.8, s32[]{:T(128)S(6)} %select_n.3, s32[]{:T(128)} %constant.9.clone.1) | dynamic-update-slice | bytes 128004 | tf_op jit(solution)/shard_map/dynamic_update_slice | solution.py:45
  18.2 48.4 %all-gather.4.cloned.1.call-done = bf16[512,1024]{1,0:T(8,128)(2,1)} async-done(((bf16[16,1024]{1,0:T(8,128)(2,1)}), bf16[512,1024]{1,0:T(8,128)(2,1)}) %all-gather.4.cloned.1.call-update) | async-done | bytes 1048592 | tf_op jit(solution)/shard_map/all_gather | solution.py:27
  66.6 1.5 multiply_reduce_fusion.2
  68.1 0.0 copy-start
  68.1 4.1 %exponential_convert_fusion.1 = bf16[1024,512]{1,0:T(8,128)(2,1)S(1)} fusion(bf16[1024,1024]{1,0:T(8,128)(2,1)} %param.7, bf16[512,1024]{1,0:T(8,128)(2,1)} %all-gather.4.cloned.1.call-done, f32[512]{0:T(512)S(1)} %multiply_reduce_fusion.2, f32[1024]{0:T(1024)S(1)} %multiply_reduce_fusion.1), kind=kOutput, calls=%fused_computation.6 | convolution fusion | flops 1077411840 | bytes 4200448 | tf_op jit(solution)/shard_map/dot_general | solution.py:13
  72.2 0.0 copy-done
  72.2 2.6 multiply_subtract_fusion.1
  74.8 0.0 copy-start.4
  74.8 61.8 %all-reduce.4 = bf16[512,1000]{0,1:T(8,128)(2,1)S(1)} all-reduce(f32[512,1000]{0,1:T(8,128)} %multiply_subtract_fusion.1), channel_id=1, replica_groups=mesh['narrow'=2,'wide'=4,'nys'=4] {'narrow','wide','nys'}, use_global_device_ids=true, to_apply=%region_2.0 | all-reduce | flops 512000 | bytes 3072000 | tf_op jit(solution)/shard_map/psum | solution.py:46
  136.6 0.0 copy-start.5
  136.6 2.4 fusion.13
  139.0 0.0 copy-done.4
  139.0 1.6 convolution_bitcast_fusion
  140.7 0.0 all-reduce.3.cloned.1.call-update
  140.7 0.2 all-gather.6.cloned.1.call-start
  140.9 0.3 all-gather.6.cloned.1.call-update
  141.3 0.0 all-gather.8.cloned.1.call-done
  141.3 53.8 %all-reduce.3.cloned.1.call-done = f32[160,1000]{1,0:T(8,128)} async-done(((f32[160,1000]{1,0:T(8,128)}), f32[160,1000]{1,0:T(8,128)}) %all-reduce.3.cloned.1.call-update) | async-done | bytes 640016 | tf_op jit(solution)/shard_map/psum | solution.py:52
  195.1 0.0 copy-done.5
  195.1 9.7 %fusion.14 = bf16[1000,2048]{1,0:T(8,128)(2,1)} fusion(f32[2048,160]{0,1:T(8,128)} %all-gather.8.cloned.1.call-done, f32[160,1000]{1,0:T(8,128)} %all-reduce.3.cloned.1.call-done, f32[160]{0:T(256)S(1)} %copy-done.5), kind=kOutput, calls=%fused_computation.22 | convolution fusion | flops 3932320000 | bytes 6047360 | tf_op jit(solution)/shard_map/dot_general | solution.py:55
  204.8 28.0 %all-gather.6.cloned.1.call-done = bf16[2048,1024]{1,0:T(8,128)(2,1)} async-done(((bf16[256,1024]{1,0:T(8,128)(2,1)}), bf16[2048,1024]{1,0:T(8,128)(2,1)}) %all-gather.6.cloned.1.call-update) | async-done | bytes 4194320 | tf_op jit(solution)/shard_map/all_gather | solution.py:28
  232.8 0.0 copy-start.3
  232.8 3.2 %multiply_reduce_fusion = f32[2048]{0:T(1024)S(1)} fusion(bf16[2048,1024]{1,0:T(8,128)(2,1)} %all-gather.6.cloned.1.call-done), kind=kLoop, calls=%fused_computation.1 | loop fusion | flops 6289408 | bytes 4202496 | tf_op jit(solution)/shard_map/reduce_sum | solution.py:16
  236.0 0.2 copy-done.3
  236.2 0.0 copy-start.2
  236.2 9.7 %exponential_convert_fusion = bf16[1024,2048]{1,0:T(8,128)(2,1)S(1)} fusion(bf16[1024,1024]{1,0:T(8,128)(2,1)} %param.7, bf16[2048,1024]{1,0:T(8,128)(2,1)S(1)} %copy-done.3, f32[2048]{0:T(1024)S(1)} %multiply_reduce_fusion, f32[1024]{0:T(1024)S(1)} %multiply_reduce_fusion.1), kind=kOutput, calls=%fused_computation | convolution fusion | flops 4309647360 | bytes 10498048 | tf_op jit(solution)/shard_map/dot_general | solution.py:13
  246.0 0.0 copy-done.2
  246.0 0.0 copy-start.1
  246.0 4.4 %fusion.30 = f32[1024,1000]{0,1:T(8,128)S(1)} fusion(bf16[1024,2048]{1,0:T(8,128)(2,1)S(1)} %exponential_convert_fusion, bf16[1000,2048]{1,0:T(8,128)(2,1)S(1)} %copy-done.2), kind=kOutput, calls=%fused_computation.38 | convolution fusion | flops 4194304000 | bytes 12386304 | tf_op jit(solution)/shard_map/dot_general | solution.py:59
  250.4 0.0 copy-done.1
  250.4 3.3 %multiply_subtract_fusion = f32[1024,1000]{0,1:T(8,128)} fusion(f32[1024,1000]{0,1:T(8,128)S(1)} %copy-done.1, f32[1024,1000]{0,1:T(8,128)S(1)} %fusion.30, bf16[1024,512]{1,0:T(8,128)(2,1)S(1)} %exponential_convert_fusion.1, bf16[512,1000]{0,1:T(8,128)(2,1)S(1)} %all-reduce.4), kind=kOutput, calls=%fused_computation.3 | convolution fusion | flops 1051648000 | bytes 14360576 | tf_op jit(solution)/shard_map/dot_general | solution.py:54
Async XLA Ops:
  6.5 60.0 %all-gather.4.cloned.1.call-start = ((), (), s32[]{:S(2)}) async-start(), calls=%async_computation | async-start | bytes 1081344 | tf_op jit(solution)/shard_map/all_gather | solution.py:27
  7.3 134.0 %all-gather.8.cloned.1.call-start = ((), (), s32[]{:S(2)}) async-start(), calls=%async_computation.3 | async-start | bytes 1474560 | tf_op jit(solution)/shard_map/all_gather | solution.py:29
  8.0 187.1 %all-reduce.3.cloned.1.call-start = ((), (), s32[]{:S(2)}) async-start(), calls=%async_computation.2 | async-start | bytes 1310720 | tf_op jit(solution)/shard_map/psum | solution.py:52
  68.1 4.1 %copy-start = (f32[1024,1000]{0,1:T(8,128)S(1)}, f32[1024,1000]{0,1:T(8,128)}, u32[]{:S(2)}) copy-start(f32[1024,1000]{0,1:T(8,128)} %param.8) | copy-start | bytes 12288004
  74.8 64.3 %copy-start.4 = (f32[256,160]{0,1:T(8,128)S(1)}, f32[256,160]{0,1:T(8,128)}, u32[]{:S(2)}) copy-start(f32[256,160]{0,1:T(8,128)} %param.12) | copy-start | bytes 491524
  136.6 58.5 %copy-start.5 = (f32[160]{0:T(256)S(1)}, f32[160]{0:T(256)}, u32[]{:S(2)}) copy-start(f32[160]{0:T(256)} %param.13) | copy-start | bytes 1924
  140.7 92.1 %all-gather.6.cloned.1.call-start = ((), (), s32[]{:S(2)}) async-start(), calls=%async_computation.1 | async-start | bytes 4718592 | tf_op jit(solution)/shard_map/all_gather | solution.py:28
  232.8 3.4 %copy-start.3 = (bf16[2048,1024]{1,0:T(8,128)(2,1)S(1)}, bf16[2048,1024]{1,0:T(8,128)(2,1)}, u32[]{:S(2)}) copy-start(bf16[2048,1024]{1,0:T(8,128)(2,1)} %all-gather.6.cloned.1.call-done) | copy-start | bytes 12582916
  236.2 9.8 %copy-start.2 = (bf16[1000,2048]{1,0:T(8,128)(2,1)S(1)}, bf16[1000,2048]{1,0:T(8,128)(2,1)}, u32[]{:S(2)}) copy-start(bf16[1000,2048]{1,0:T(8,128)(2,1)} %fusion.14) | copy-start | bytes 12288004
  246.0 4.5 %copy-start.1 = (f32[1024,1000]{0,1:T(8,128)S(1)}, f32[1024,1000]{0,1:T(8,128)}, u32[]{:S(2)}) copy-start(f32[1024,1000]{0,1:T(8,128)} %param.8) | copy-start | bytes 12288004
Sparse Core Ops, SparseCore 0:
  10.2 56.3 all-gather.3
  68.4 26.0 all-gather.7
  140.8 54.1 all-reduce.2
  196.8 35.9 all-gather.5
where the time goes:
time: 261 us; the launch traced here: 260 us
  waiting for transfers between devices  132 us (51%)
  blocking collectives  61.8 us (24%)
  matrix products  37.9 us (15%)
  between operations  13.3 us (5%)
  other arithmetic  8.02 us (3%)
  local copies, waits for them, and re-layouts  7.05 us (3%)
    psum x1, blocking collectives, per_device(): lax.psum(partial_value - placed, ('narrow', 'wide', 'nys'))  61.8 us
    psum x1, waiting for transfers between devices, per_device(): projected = lax.psum(local_proj, ('narrow', 'nys'))  53.8 us
    all_gather x1, waiting for transfers between devices, per_device(): lax.all_gather(batch_points, ('narrow', 'wide', 'nys'), axis=0, tiled=True)  48.4 us
    all_gather x1, waiting for transfers between devices, per_device(): lax.all_gather(nystrom_points, ('narrow', 'nys'), axis=0, tiled=True)  28 us
    dot_general x2, matrix products, kernel_with(): lax.dot_general(left, right, (((1,), (1,)), ((), ())), preferred_element_...  13.8 us
    dot_general x1, matrix products, per_device(): jnp.dot(vectors_full, scaled_proj, precision=lax.Precision.HIGHEST)  9.72 us
    dynamic_update_slice x1, local copies, waits for them, and re-layouts, per_device(): lax.dynamic_update_slice(jnp.zeros_like(partial_value), labels, (offset,...  5.52 us
  transfers between devices with their start and end apart: 4, of which 3 were waited for; matrix products, arithmetic and copies ran while one was open for 12% of the time, Pallas kernels for 0%

commit v1 on v0

--- a/solution.py
+++ b/solution.py
@@ -43,7 +43,9 @@
     rows = labels.shape[0]
     offset = lax.axis_index(("narrow", "wide", "nys")) * rows
     placed = lax.dynamic_update_slice(jnp.zeros_like(partial_value), labels, (offset, jnp.int32(0)))
-    residual = lax.psum(partial_value - placed, ("narrow", "wide", "nys")).astype(jnp.bfloat16)
+    residual = lax.psum(lax.psum(partial_value - placed, ("wide", "nys")), "narrow").astype(
+        jnp.bfloat16
+    )
     k_nystrom = kernel_with(nystrom_points, squares(nystrom_points), batch_all)
     pulled = jnp.dot(k_nystrom, residual, preferred_element_type=jnp.float32)
     local_proj = lax.dot_general(

time: 261 us -> 349 us (1.34)
  waiting for transfers between devices: 132 us -> 228 us
  blocking collectives: 61.8 us -> 50.1 us
    psum x0 -> x1, waiting for transfers between devices: none -> 95.3 us  [per_device(): lax.psum(partial_value - placed, ('wide', 'nys'))]
    psum x1, blocking collectives: 61.8 us -> 50.1 us  [per_device(): lax.psum(lax.psum(partial_value - placed, ('wide', 'nys')), 'narrow')]
  transfers between devices with their start and end apart: 4 -> 5, of which waited for: 3 -> 4; matrix products, arithmetic and copies ran while one was open for 12% -> 7% of each run, Pallas kernels for 0% -> 0%
where the time goes in v1:
time: 349 us
  waiting for transfers between devices  228 us (65%)
  blocking collectives  50.1 us (14%)
  matrix products  40 us (11%)
  between operations  15.2 us (4%)
  other arithmetic  8.02 us (2%)
  local copies, waits for them, and re-layouts  7.05 us (2%)
    psum x1, waiting for transfers between devices, per_device(): lax.psum(partial_value - placed, ('wide', 'nys'))  95.3 us
    psum x1, waiting for transfers between devices, per_device(): projected = lax.psum(local_proj, ('narrow', 'nys'))  52.9 us
    all_gather x1, waiting for transfers between devices, per_device(): lax.all_gather(batch_points, ('narrow', 'wide', 'nys'), axis=0, tiled=True)  50.4 us
    psum x1, blocking collectives, per_device(): lax.psum(lax.psum(partial_value - placed, ('wide', 'nys')), 'narrow')  50.1 us
    all_gather x1, waiting for transfers between devices, per_device(): lax.all_gather(nystrom_points, ('narrow', 'nys'), axis=0, tiled=True)  27.9 us
    dot_general x2, matrix products, kernel_with(): lax.dot_general(left, right, (((1,), (1,)), ((), ())), preferred_element_...  13.8 us
    dot_general x1, matrix products, per_device(): jnp.dot(vectors_full, scaled_proj, precision=lax.Precision.HIGHEST)  9.72 us
  transfers between devices with their start and end apart: 5, of which 4 were waited for; matrix products, arithmetic and copies ran while one was open for 7% of the time, Pallas kernels for 0%

profile of v1, /device:TPU:0, one launch (start us, length us, event | category | flops | bytes accessed | tf_op | source)
XLA Modules:
  0.0 348.8 jit_solution(4980144249862710173)
XLA Ops:
  7.4 0.0 all-gather.4.cloned.1.call-start
  7.4 0.7 all-gather.4.cloned.1.call-update
  8.1 0.0 all-reduce.4.cloned.1.call-start
  8.1 1.0 copy.8
  9.2 0.2 broadcast_in_dim.2
  9.4 5.5 %dynamic_update_slice.3 = f32[512,1000]{0,1:T(8,128)S(1)} dynamic-update-slice(f32[512,1000]{0,1:T(8,128)S(1)} %broadcast_in_dim.2, f32[16,1000]{0,1:T(8,128)S(1)} %copy.8, s32[]{:T(128)S(6)} %select_n.3, s32[]{:T(128)} %constant.9.clone.1) | dynamic-update-slice | bytes 128004 | tf_op jit(solution)/shard_map/dynamic_update_slice | solution.py:45
  15.0 2.1 multiply_reduce_fusion.1
  17.0 50.4 %all-gather.4.cloned.1.call-done = bf16[512,1024]{1,0:T(8,128)(2,1)} async-done(((bf16[16,1024]{1,0:T(8,128)(2,1)}), bf16[512,1024]{1,0:T(8,128)(2,1)}) %all-gather.4.cloned.1.call-update) | async-done | bytes 1048592 | tf_op jit(solution)/shard_map/all_gather | solution.py:27
  67.4 1.5 multiply_reduce_fusion.2
  68.9 0.0 copy-start
  68.9 4.1 %exponential_convert_fusion.1 = bf16[1024,512]{1,0:T(8,128)(2,1)S(1)} fusion(bf16[1024,1024]{1,0:T(8,128)(2,1)} %param.7, bf16[512,1024]{1,0:T(8,128)(2,1)} %all-gather.4.cloned.1.call-done, f32[512]{0:T(512)S(1)} %multiply_reduce_fusion.2, f32[1024]{0:T(1024)S(1)} %multiply_reduce_fusion.1), kind=kOutput, calls=%fused_computation.6 | convolution fusion | flops 1077411840 | bytes 4200448 | tf_op jit(solution)/shard_map/dot_general | solution.py:13
  73.0 0.0 copy-done
  73.0 2.6 multiply_subtract_fusion.1
  75.6 0.0 copy-start.4
  75.6 0.0 all-reduce.4.cloned.1.call-update
  75.6 0.0 copy-start.5
  75.6 0.0 all-gather.8.cloned.1.call-start
  75.7 0.5 all-gather.8.cloned.1.call-update
  76.2 0.0 all-reduce.6.cloned.1.call-start
  76.3 1.2 multiply_reduce_fusion.3
  77.5 95.3 %all-reduce.4.cloned.1.call-done = f32[512,1000]{0,1:T(8,128)} async-done(((f32[512,1000]{0,1:T(8,128)}), f32[512,1000]{0,1:T(8,128)}) %all-reduce.4.cloned.1.call-update) | async-done | bytes 2048016 | tf_op jit(solution)/shard_map/psum | solution.py:46
  172.8 50.1 %all-reduce.7 = bf16[512,1000]{0,1:T(8,128)(2,1)S(1)} all-reduce(f32[512,1000]{0,1:T(8,128)} %all-reduce.4.cloned.1.call-done), channel_id=1, replica_groups=mesh['narrow'=2,'wide'=4,'nys'=4] {'narrow'}, use_global_device_ids=true, to_apply=%region_3.0 | all-reduce | flops 512000 | bytes 3072000 | tf_op jit(solution)/shard_map/psum | solution.py:46
  222.9 0.0 copy-done.4
  222.9 0.0 copy-start.6
  222.9 3.2 fusion.13
  226.2 0.0 copy-done.5
  226.2 2.9 convolution_bitcast_fusion
  229.0 0.0 all-reduce.6.cloned.1.call-update
  229.1 0.2 all-gather.6.cloned.1.call-start
  229.3 0.3 all-gather.6.cloned.1.call-update
  229.6 0.0 all-gather.8.cloned.1.call-done
  229.7 52.9 %all-reduce.6.cloned.1.call-done = f32[160,1000]{1,0:T(8,128)} async-done(((f32[160,1000]{1,0:T(8,128)}), f32[160,1000]{1,0:T(8,128)}) %all-reduce.6.cloned.1.call-update) | async-done | bytes 640016 | tf_op jit(solution)/shard_map/psum | solution.py:54
  282.6 0.0 copy-done.6
  282.6 9.7 %fusion.14 = bf16[1000,2048]{1,0:T(8,128)(2,1)} fusion(f32[2048,160]{0,1:T(8,128)} %all-gather.8.cloned.1.call-done, f32[160,1000]{1,0:T(8,128)} %all-reduce.6.cloned.1.call-done, f32[160]{0:T(256)S(1)} %copy-done.6), kind=kOutput, calls=%fused_computation.22 | convolution fusion | flops 3932320000 | bytes 6047360 | tf_op jit(solution)/shard_map/dot_general | solution.py:57
  292.3 27.9 %all-gather.6.cloned.1.call-done = bf16[2048,1024]{1,0:T(8,128)(2,1)} async-done(((bf16[256,1024]{1,0:T(8,128)(2,1)}), bf16[2048,1024]{1,0:T(8,128)(2,1)}) %all-gather.6.cloned.1.call-update) | async-done | bytes 4194320 | tf_op jit(solution)/shard_map/all_gather | solution.py:28
  320.2 0.0 copy-start.3
  320.2 3.2 multiply_reduce_fusion
  323.4 0.2 copy-done.3
  323.7 0.0 copy-start.2
  323.7 9.7 %exponential_convert_fusion = bf16[1024,2048]{1,0:T(8,128)(2,1)S(1)} fusion(bf16[1024,1024]{1,0:T(8,128)(2,1)} %param.7, bf16[2048,1024]{1,0:T(8,128)(2,1)S(1)} %copy-done.3, f32[2048]{0:T(1024)S(1)} %multiply_reduce_fusion, f32[1024]{0:T(1024)S(1)} %multiply_reduce_fusion.1), kind=kOutput, calls=%fused_computation | convolution fusion | flops 4309647360 | bytes 10498048 | tf_op jit(solution)/shard_map/dot_general | solution.py:13
  333.4 0.0 copy-done.2
  333.4 0.0 copy-start.1
  333.4 4.4 %fusion.30 = f32[1024,1000]{0,1:T(8,128)S(1)} fusion(bf16[1024,2048]{1,0:T(8,128)(2,1)S(1)} %exponential_convert_fusion, bf16[1000,2048]{1,0:T(8,128)(2,1)S(1)} %copy-done.2), kind=kOutput, calls=%fused_computation.38 | convolution fusion | flops 4194304000 | bytes 12386304 | tf_op jit(solution)/shard_map/dot_general | solution.py:61
  337.9 0.0 copy-done.1
  337.9 3.3 multiply_subtract_fusion
Async XLA Ops:
  7.4 60.0 %all-gather.4.cloned.1.call-start = ((), (), s32[]{:S(2)}) async-start(), calls=%async_computation | async-start | bytes 1081344 | tf_op jit(solution)/shard_map/all_gather | solution.py:27
  8.1 164.7 %all-reduce.4.cloned.1.call-start = ((), (), s32[]{:S(2)}) async-start(), calls=%async_computation.1 | async-start | bytes 4096000 | tf_op jit(solution)/shard_map/psum | solution.py:46
  68.9 4.1 %copy-start = (f32[1024,1000]{0,1:T(8,128)S(1)}, f32[1024,1000]{0,1:T(8,128)}, u32[]{:S(2)}) copy-start(f32[1024,1000]{0,1:T(8,128)} %param.8) | copy-start | bytes 12288004
  75.6 147.3 %copy-start.4 = (bf16[256,1024]{1,0:T(8,128)(2,1)S(1)}, bf16[256,1024]{1,0:T(8,128)(2,1)}, u32[]{:S(2)}) copy-start(bf16[256,1024]{1,0:T(8,128)(2,1)} %param.11) | copy-start | bytes 1572868
  75.6 150.5 %copy-start.5 = (f32[256,160]{0,1:T(8,128)S(1)}, f32[256,160]{0,1:T(8,128)}, u32[]{:S(2)}) copy-start(f32[256,160]{0,1:T(8,128)} %param.12) | copy-start | bytes 491524
  75.6 154.0 %all-gather.8.cloned.1.call-start = ((), (), s32[]{:S(2)}) async-start(), calls=%async_computation.4 | async-start | bytes 1474560 | tf_op jit(solution)/shard_map/all_gather | solution.py:29
  76.2 206.3 %all-reduce.6.cloned.1.call-start = ((), (), s32[]{:S(2)}) async-start(), calls=%async_computation.3 | async-start | bytes 1310720 | tf_op jit(solution)/shard_map/psum | solution.py:54
  222.9 59.6 %copy-start.6 = (f32[160]{0:T(256)S(1)}, f32[160]{0:T(256)}, u32[]{:S(2)}) copy-start(f32[160]{0:T(256)} %param.13) | copy-start | bytes 1924
  229.1 91.2 %all-gather.6.cloned.1.call-start = ((), (), s32[]{:S(2)}) async-start(), calls=%async_computation.2 | async-start | bytes 4718592 | tf_op jit(solution)/shard_map/all_gather | solution.py:28
  320.2 3.4 copy-start.3
  323.7 9.8 %copy-start.2 = (bf16[1000,2048]{1,0:T(8,128)(2,1)S(1)}, bf16[1000,2048]{1,0:T(8,128)(2,1)}, u32[]{:S(2)}) copy-start(bf16[1000,2048]{1,0:T(8,128)(2,1)} %fusion.14) | copy-start | bytes 12288004
  333.4 4.5 %copy-start.1 = (f32[1024,1000]{0,1:T(8,128)S(1)}, f32[1024,1000]{0,1:T(8,128)}, u32[]{:S(2)}) copy-start(f32[1024,1000]{0,1:T(8,128)} %param.8) | copy-start | bytes 12288004
Sparse Core Ops, SparseCore 0:
  11.0 56.3 all-gather.3
  75.8 97.0 all-reduce.3
Sparse Core Ops, SparseCore 1:
  78.0 23.8 all-gather.7
  229.2 53.4 all-reduce.5
  284.3 35.8 all-gather.5
